TPU v7x, 128 devices: a whole 4x4x4 slice. The times are simulated.
128 devices in a mesh: req: 16 (over z, x_hi, core), head: 8 (over y, x_lo).
Axes of the slice: x: 4 (x_hi: 2, x_lo: 2; x = x_hi * 2 + x_lo), y: 4, z: 4, core: 2. Of those that a mesh axis runs over, the one named last changes fastest.
Arguments:
- hidden_in: bfloat16 [128, 8192], P('head', 'req'), may hold values from -40 to 40
- attn_gain: bfloat16 [8192], P('req'), may hold values from 0.5 to 1.5
- w_qkv: bfloat16 [8192, 10240], P('req', 'head'), may hold values from -0.0625 to 0.0625
- w_out: bfloat16 [8192, 8192], P('head', 'req'), may hold values from -0.0625 to 0.0625
- k_cache: bfloat16 [128, 4096, 1024], P('req', None, 'head'), may hold values from -400 to 400
- v_cache: bfloat16 [128, 4096, 1024], P('req', None, 'head'), may hold values from -6 to 6
- lengths: int32 [128], P('req'), may hold values from 1 to 4096, 135168 in all
Outputs:
- hidden_out: bfloat16 [128, 8192], P('head', 'req')
Inputs may be any that keep to these rules, and one draw needn't show every extreme that they name: One request holds exactly 4096 tokens; the lengths add up to 135168.
All inputs are finite; a program needn't handle non-finite values. No bound on the sum of `lengths` on one device may be relied on, other than what follows from the above.
Results may differ from a plain program's by a relative error of at most 0.0055.
Values may be sent and summed in bfloat16 or wider, within the bound.
A program may use at most 64 MiB of HBM per device.

v0:
```python
import jax
import jax.numpy as jnp
from jax import lax
from jax.sharding import PartitionSpec as P

D = 8192
GROUP = 8
HD = 128
epsilon = 1e-05
rope_base = 500000.0


def rotate(vectors, positions):
    halfway = vectors.shape[-1] // 2
    frequency = jnp.exp(
        -jnp.log(rope_base) * 2.0 * jnp.arange(halfway, dtype=jnp.float32) / vectors.shape[-1]
    )
    angles = positions.astype(jnp.float32)[:, None] * frequency[None, :]
    target_shape = (angles.shape[0],) + (1,) * (vectors.ndim - 2) + (halfway,)
    cosine = jnp.cos(angles).reshape(target_shape)
    sine_part = jnp.sin(angles).reshape(target_shape)
    first = vectors[..., :halfway]
    second = vectors[..., halfway:]
    return jnp.concatenate(
        [first * cosine - second * sine_part, second * cosine + first * sine_part], axis=-1
    )


def own_part(own_score, running, totals, new_values):
    own_prob = lax.optimization_barrier(
        (jnp.exp(own_score - running) / totals).astype(jnp.bfloat16)
    )
    return own_prob.astype(jnp.float32)[..., None] * new_values.astype(jnp.float32)[:, :, None, :]


def attend_padded(queries, new_keys, new_values, cached_keys, cached_values, lengths, factor):
    slots = cached_keys.shape[1]
    inside = jnp.arange(slots, dtype=jnp.int32)[None, :] < lengths[:, None]
    scores = (
        jnp.einsum("rkgd,rpkd->rkgp", queries, cached_keys, preferred_element_type=jnp.float32)
        * factor
    )
    scores = jnp.where(inside[:, None, None, :], scores, -1e30)
    own_score = (
        jnp.einsum("rkgd,rkd->rkg", queries, new_keys, preferred_element_type=jnp.float32) * factor
    )
    running = jnp.maximum(jnp.max(scores, axis=3), own_score)
    weights = jnp.where(inside[:, None, None, :], jnp.exp(scores - running[..., None]), 0.0)
    totals = jnp.sum(weights, axis=3) + jnp.exp(own_score - running)
    probs = (weights / totals[..., None]).astype(jnp.bfloat16)
    mixed = jnp.einsum("rkgp,rpkd->rkgd", probs, cached_values, preferred_element_type=jnp.float32)
    mixed = mixed + own_part(own_score, running, totals, new_values)
    return mixed.astype(jnp.bfloat16)


def local(hidden_in, attn_gain, w_qkv, w_out, k_cache, v_cache, lengths):
    states = hidden_in.astype(jnp.float32)
    every_row = lax.all_gather(hidden_in, "head", axis=0, tiled=True).astype(jnp.float32)
    scaled = (every_row * attn_gain.astype(jnp.float32)[None, :]).astype(jnp.bfloat16)
    partial_square = jnp.sum(every_row * every_row, axis=1)
    partial = jnp.dot(scaled, w_qkv, preferred_element_type=jnp.float32)
    columns = partial.shape[1]
    packed = jnp.concatenate(
        [partial, jnp.broadcast_to(partial_square[:, None], (partial.shape[0], 128))], axis=1
    )
    summed = lax.psum_scatter(packed, "req", scatter_dimension=0, tiled=True)
    mean_square = summed[:, columns] / D
    own_count = k_cache.shape[0]
    slots = k_cache.shape[1]
    local_heads = k_cache.shape[2] // HD
    projected = summed[:, :columns] * lax.rsqrt(mean_square + epsilon)[:, None]
    projected = projected.reshape(own_count, local_heads, GROUP + 2, HD)
    queries = rotate(projected[:, :, :GROUP], lengths).astype(jnp.bfloat16)
    new_keys = rotate(projected[:, :, GROUP], lengths).astype(jnp.bfloat16)
    new_values = projected[:, :, GROUP + 1].astype(jnp.bfloat16)
    cached_keys = k_cache.reshape(own_count, slots, local_heads, HD)
    cached_values = v_cache.reshape(own_count, slots, local_heads, HD)
    factor = HD ** (-0.5)
    attended = attend_padded(
        queries, new_keys, new_values, cached_keys, cached_values, lengths, factor
    )
    flat_rows = attended.reshape(own_count, local_heads * GROUP * HD)
    gathered = lax.all_gather(flat_rows, "req", axis=0, tiled=True)
    output = lax.psum_scatter(
        jnp.dot(gathered, w_out, preferred_element_type=jnp.float32),
        "head",
        scatter_dimension=0,
        tiled=True,
    )
    return (states + output).astype(jnp.bfloat16)


def solution(mesh):
    return jax.shard_map(
        local,
        mesh=mesh,
        in_specs=(
            P("head", "req"),
            P("req"),
            P("req", "head"),
            P("head", "req"),
            P("req", None, "head"),
            P("req", None, "head"),
            P("req"),
        ),
        out_specs=P("head", "req"),
        check_vma=False,
    )
```

profile of v0, /device:TPU:0, one launch (start us, length us, event | category | flops | bytes accessed | tf_op | source)
XLA Modules:
  0.0 255.5 jit_solution(280369030877171777)
XLA Ops:
  6.5 0.0 copy-start
  6.5 0.0 all-reduce.3.cloned.1.call-start
  6.5 29.1 %all_gather.6 = bf16[128,512]{1,0:T(8,128)(2,1)S(1)} all-gather(bf16[16,512]{1,0:T(8,128)(2,1)} %param.7), channel_id=1, replica_groups=mesh['req'=16,'head'=8] {'head'}, dimensions={0}, use_global_device_ids=true | all-gather | bytes 147456 | tf_op jit(solution)/shard_map/all_gather | solution.py:58
  35.6 0.7 convert_element_type.53
  36.3 0.1 fusion.9
  36.4 0.0 copy-done
  36.4 0.3 fusion.10
  36.7 0.1 broadcast_in_dim.21
  36.8 0.9 pad_maximum_fusion
  37.7 0.0 all-reduce.3.cloned.1.call-update
  37.8 0.0 reduce-scatter.2.cloned.1.call-start
  37.8 0.7 convert_element_type.55
  38.5 1.2 dynamic-slice
  40.4 0.1 multiply_cosine_fusion.1
  40.5 0.7 iota_compare_fusion
  41.2 137.7 %all-reduce.3.cloned.1.call-done = f32[128,1408]{1,0:T(8,128)} async-done(((f32[128,1408]{1,0:T(8,128)}), f32[128,1408]{1,0:T(8,128)}) %all-reduce.3.cloned.1.call-update) | async-done | bytes 720912
  178.9 0.0 copy-start.1
  178.9 1.0 fusion.26
  179.9 1.1 fusion.13
  181.0 0.1 fusion.38
  181.1 0.1 fusion.33
  181.2 0.1 maximum_bitcast_fusion
  181.3 0.2 fusion.27
  181.5 5.8 %fusion.39 = (f32[8,8]{1,0:T(8,128)S(1)}, f32[8,8,4096]{2,1,0:T(8,128)S(1)}) fusion(bf16[8,4096,128]{2,1,0:T(8,128)(2,1)} %param.11, bf16[8,8,64]{2,1,0:T(8,128)(2,1)S(1)} %get-tuple-element.6, bf16[8,8,64]{2,1,0:T(8,128)(2,1)S(1)} %get-tuple-element.5, pred[8,4096]{1,0:T(8,128)(4,1)S(1)} %iota_compare_fusion), kind=kOutput, calls=%fused_computation.65 | convolution fusion | flops 67928000 | bytes 9486592 | tf_op jit(solution)/shard_map/rkgd,rpkd->rkgp/dot_general | solution.py:40
  187.3 0.4 fusion.3
  187.7 0.0 copy-done.1
  187.7 0.0 copy-start.2
  187.7 0.0 copy-start.3
  187.8 1.3 fusion.2
  189.1 20.8 %all_gather.7 = bf16[128,1024]{1,0:T(8,128)(2,1)S(1)} all-gather(bf16[8,1024]{1,0:T(8,128)(2,1)S(1)} %bitcast.37), channel_id=1, replica_groups=mesh['req'=16,'head'=8] {'req'}, dimensions={0}, use_global_device_ids=true | all-gather | bytes 278528 | tf_op jit(solution)/shard_map/all_gather | solution.py:83
  209.9 0.0 copy-done.2
  209.9 1.0 fusion.40
  210.9 0.0 reduce-scatter.2.cloned.1.call-update
  210.9 36.3 %reduce-scatter.2.cloned.1.call-done = f32[16,512]{1,0:T(8,128)} async-done(((f32[128,512]{1,0:T(8,128)}), f32[16,512]{1,0:T(8,128)}) %reduce-scatter.2.cloned.1.call-update) | async-done | bytes 32784 | tf_op jit(solution)/shard_map/reduce_scatter | solution.py:84
  247.3 0.0 copy-done.3
  247.3 1.4 add_convert_fusion
  (8 shorter events, 0.1 us)
Async XLA Ops:
  6.5 29.9 %copy-start = (bf16[512,1280]{1,0:T(8,128)(2,1)S(1)}, bf16[512,1280]{1,0:T(8,128)(2,1)}, u32[]{:S(2)}) copy-start(bf16[512,1280]{1,0:T(8,128)(2,1)} %param.9) | copy-start | bytes 3932164
  6.5 172.4 %all-reduce.3.cloned.1.call-start = ((), (), s32[]{:S(2)}) async-start(), calls=%async_computation.2 | async-start | bytes 1441792
  37.8 209.5 %reduce-scatter.2.cloned.1.call-start = ((), (), s32[]{:S(2)}) async-start(), calls=%async_computation.1 | async-start | bytes 294912 | tf_op jit(solution)/shard_map/reduce_scatter | solution.py:84
  178.9 8.8 %copy-start.1 = (bf16[8,4096,128]{2,1,0:T(8,128)(2,1)S(1)}, bf16[8,4096,128]{2,1,0:T(8,128)(2,1)}, u32[]{:S(2)}) copy-start(bf16[8,4096,128]{2,1,0:T(8,128)(2,1)} %param.12) | copy-start | bytes 25165828
  187.7 22.2 %copy-start.2 = (bf16[1024,512]{1,0:T(8,128)(2,1)S(1)}, bf16[1024,512]{1,0:T(8,128)(2,1)}, u32[]{:S(2)}) copy-start(bf16[1024,512]{1,0:T(8,128)(2,1)} %param.10) | copy-start | bytes 3145732
  187.7 59.5 %copy-start.3 = (bf16[16,512]{1,0:T(8,128)(2,1)S(1)}, bf16[16,512]{1,0:T(8,128)(2,1)}, u32[]{:S(2)}) copy-start(bf16[16,512]{1,0:T(8,128)(2,1)} %param.7) | copy-start | bytes 49156
Sparse Core Ops, SparseCore 0:
  37.9 140.9 all-reduce.2
  211.1 36.1 reduce-scatter.1
where the time goes:
time: 256 us; the launch traced here: 255 us
  waiting for transfers between devices  174 us (68%)
  blocking collectives  49.8 us (19%)
  between operations  14.1 us (6%)
  matrix products  8.67 us (3%)
  other arithmetic  7.34 us (3%)
    unnamed x3, waiting for transfers between devices  138 us
    reduce_scatter x1, waiting for transfers between devices, local(): lax.psum_scatter(jnp.dot(gathered, w_out, preferred_element_type=jnp.floa...  36.3 us
    all_gather x1, blocking collectives, local(): lax.all_gather(hidden_in, 'head', axis=0, tiled=True).astype(jnp.float32)  29.1 us
    all_gather x1, blocking collectives, local(): gathered = lax.all_gather(flat_rows, 'req', axis=0, tiled=True)  20.8 us
    dot_general x1, matrix products, attend_padded(): jnp.einsum('rkgd,rpkd->rkgp', queries, cached_keys, preferred_element_typ...  5.77 us
  transfers between devices with their start and end apart: 2, of which 2 were waited for; matrix products, arithmetic and copies ran while one was open for 1% of the time, Pallas kernels for 0%

commit v1 on v0

--- a/solution.py
+++ b/solution.py
@@ -55,7 +55,9 @@
 
 def local(hidden_in, attn_gain, w_qkv, w_out, k_cache, v_cache, lengths):
     states = hidden_in.astype(jnp.float32)
-    every_row = lax.all_gather(hidden_in, "head", axis=0, tiled=True).astype(jnp.float32)
+    every_row = jnp.concatenate(
+        lax.all_to_all(jnp.stack([hidden_in] * lax.axis_size("head")), "head", 0, 0), axis=0
+    ).astype(jnp.float32)
     scaled = (every_row * attn_gain.astype(jnp.float32)[None, :]).astype(jnp.bfloat16)
     partial_square = jnp.sum(every_row * every_row, axis=1)
     partial = jnp.dot(scaled, w_qkv, preferred_element_type=jnp.float32)

time: 256 us -> 238 us (0.930)
  blocking collectives: 49.8 us -> 20.8 us
  starting transfers between devices: 0.04 us -> 5.56 us
  waiting for transfers between devices: 174 us -> 178 us
    all_gather x1 -> x0, blocking collectives: 29.1 us -> none  [local(): lax.all_gather(hidden_in, 'head', axis=0, tiled=True).astype(jnp.float32)]
    all_to_all x0 -> x1, starting transfers between devices: none -> 5.48 us  [local(): lax.all_to_all(jnp.stack([hidden_in] * lax.axis_size('head')), 'head', 0, 0)]
    all_to_all x0 -> x1, waiting for transfers between devices: none -> 3.29 us  [local(): lax.all_to_all(jnp.stack([hidden_in] * lax.axis_size('head')), 'head', 0, 0)]
  transfers between devices with their start and end apart: 2 -> 3, of which waited for: 2 -> 3; matrix products, arithmetic and copies ran while one was open for 1% -> 1% of each run, Pallas kernels for 0% -> 0%
where the time goes in v1:
time: 238 us
  waiting for transfers between devices  178 us (75%)
  blocking collectives  20.8 us (9%)
  between operations  14.2 us (6%)
  matrix products  8.67 us (4%)
  other arithmetic  7.34 us (3%)
  starting transfers between devices  5.56 us (2%)
  local copies, waits for them, and re-layouts  2.98 us (1%)
    unnamed x3, waiting for transfers between devices  139 us
    reduce_scatter x1, waiting for transfers between devices, local(): lax.psum_scatter(jnp.dot(gathered, w_out, preferred_element_type=jnp.floa...  36.3 us
    all_gather x1, blocking collectives, local(): gathered = lax.all_gather(flat_rows, 'req', axis=0, tiled=True)  20.8 us
    dot_general x1, matrix products, attend_padded(): jnp.einsum('rkgd,rpkd->rkgp', queries, cached_keys, preferred_element_typ...  5.77 us
    all_to_all x1, starting transfers between devices, local(): lax.all_to_all(jnp.stack([hidden_in] * lax.axis_size('head')), 'head', 0, 0)  5.48 us
  transfers between devices with their start and end apart: 3, of which 3 were waited for; matrix products, arithmetic and copies ran while one was open for 1% of the time, Pallas kernels for 0%

profile of v1, /device:TPU:0, one launch (start us, length us, event | category | flops | bytes accessed | tf_op | source)
XLA Modules:
  0.0 237.7 jit_solution(4649466943314515733)
XLA Ops:
  6.5 0.0 copy-start
  6.5 1.5 stack.2
  8.0 5.5 %all-to-all-start = ((bf16[8,16,512]{2,1,0:T(8,128)(2,1)}), bf16[8,16,512]{2,1,0:T(8,128)(2,1)S(1)}, u32[]{:S(2)}, u32[]{:S(2)}) async-start(bf16[8,16,512]{2,1,0:T(8,128)(2,1)} %stack.2), calls=%async_computation | async-start | bytes 262144 | tf_op jit(solution)/shard_map/all_to_all | solution.py:59
  13.5 0.0 all-reduce.3.cloned.1.call-start
  13.6 0.7 convert_element_type.60
  14.2 0.7 convert_element_type.63
  14.9 1.2 dynamic-slice
  16.8 0.1 multiply_cosine_fusion.1
  16.9 3.3 %all-to-all-done = bf16[8,16,512]{2,1,0:T(8,128)(2,1)S(1)} async-done(((bf16[8,16,512]{2,1,0:T(8,128)(2,1)}), bf16[8,16,512]{2,1,0:T(8,128)(2,1)S(1)}, u32[]{:S(2)}, u32[]{:S(2)}) %all-to-all-start) | async-done | bytes 131104 | tf_op jit(solution)/shard_map/all_to_all | solution.py:59
  20.2 0.1 multiply_reduce_fusion
  20.3 0.1 broadcast_in_dim.23
  20.4 0.0 copy-done
  20.4 0.3 fusion.36
  20.8 0.1 broadcast_in_dim.24
  20.9 0.9 pad_maximum_fusion
  21.8 0.0 all-reduce.3.cloned.1.call-update
  21.8 0.0 reduce-scatter.2.cloned.1.call-start
  21.9 0.7 iota_compare_fusion
  22.6 138.6 %all-reduce.3.cloned.1.call-done = f32[128,1408]{1,0:T(8,128)} async-done(((f32[128,1408]{1,0:T(8,128)}), f32[128,1408]{1,0:T(8,128)}) %all-reduce.3.cloned.1.call-update) | async-done | bytes 720912
  161.2 0.0 copy-start.1
  161.2 1.0 fusion.22
  162.2 1.1 fusion.9
  163.3 0.1 fusion.34
  163.3 0.1 fusion.29
  163.5 0.1 maximum_bitcast_fusion
  163.6 0.2 fusion.23
  163.8 5.8 %fusion.35 = (f32[8,8]{1,0:T(8,128)S(1)}, f32[8,8,4096]{2,1,0:T(8,128)S(1)}) fusion(bf16[8,4096,128]{2,1,0:T(8,128)(2,1)} %param.11, bf16[8,8,64]{2,1,0:T(8,128)(2,1)S(1)} %get-tuple-element.6, bf16[8,8,64]{2,1,0:T(8,128)(2,1)S(1)} %get-tuple-element.5, pred[8,4096]{1,0:T(8,128)(4,1)S(1)} %iota_compare_fusion), kind=kOutput, calls=%fused_computation.62 | convolution fusion | flops 67928000 | bytes 9486592 | tf_op jit(solution)/shard_map/rkgd,rpkd->rkgp/dot_general | solution.py:40
  169.5 0.4 fusion.3
  170.0 0.0 copy-done.1
  170.0 0.0 copy-start.2
  170.0 0.0 copy-start.3
  170.0 1.3 fusion.2
  171.4 20.8 %all_gather.3 = bf16[128,1024]{1,0:T(8,128)(2,1)S(1)} all-gather(bf16[8,1024]{1,0:T(8,128)(2,1)S(1)} %bitcast.42), channel_id=1, replica_groups=mesh['req'=16,'head'=8] {'req'}, dimensions={0}, use_global_device_ids=true | all-gather | bytes 278528 | tf_op jit(solution)/shard_map/all_gather | solution.py:85
  192.2 0.0 copy-done.2
  192.2 1.0 fusion.37
  193.2 0.0 reduce-scatter.2.cloned.1.call-update
  193.2 36.3 %reduce-scatter.2.cloned.1.call-done = f32[16,512]{1,0:T(8,128)} async-done(((f32[128,512]{1,0:T(8,128)}), f32[16,512]{1,0:T(8,128)}) %reduce-scatter.2.cloned.1.call-update) | async-done | bytes 32784 | tf_op jit(solution)/shard_map/reduce_scatter | solution.py:86
  229.5 0.0 copy-done.3
  229.5 1.4 add_convert_fusion
  (9 shorter events, 0.1 us)
Async XLA Ops:
  6.5 13.9 %copy-start = (bf16[512,1280]{1,0:T(8,128)(2,1)S(1)}, bf16[512,1280]{1,0:T(8,128)(2,1)}, u32[]{:S(2)}) copy-start(bf16[512,1280]{1,0:T(8,128)(2,1)} %param.9) | copy-start | bytes 3932164
  8.0 12.2 %all-to-all-start = ((bf16[8,16,512]{2,1,0:T(8,128)(2,1)}), bf16[8,16,512]{2,1,0:T(8,128)(2,1)S(1)}, u32[]{:S(2)}, u32[]{:S(2)}) async-start(bf16[8,16,512]{2,1,0:T(8,128)(2,1)} %stack.2), calls=%async_computation | async-start | bytes 262144 | tf_op jit(solution)/shard_map/all_to_all | solution.py:59
  13.5 147.7 %all-reduce.3.cloned.1.call-start = ((), (), s32[]{:S(2)}) async-start(), calls=%async_computation.3 | async-start | bytes 1441792
  21.8 207.7 %reduce-scatter.2.cloned.1.call-start = ((), (), s32[]{:S(2)}) async-start(), calls=%async_computation.2 | async-start | bytes 294912 | tf_op jit(solution)/shard_map/reduce_scatter | solution.py:86
  161.2 8.8 %copy-start.1 = (bf16[8,4096,128]{2,1,0:T(8,128)(2,1)S(1)}, bf16[8,4096,128]{2,1,0:T(8,128)(2,1)}, u32[]{:S(2)}) copy-start(bf16[8,4096,128]{2,1,0:T(8,128)(2,1)} %param.12) | copy-start | bytes 25165828
  170.0 22.2 %copy-start.2 = (bf16[1024,512]{1,0:T(8,128)(2,1)S(1)}, bf16[1024,512]{1,0:T(8,128)(2,1)}, u32[]{:S(2)}) copy-start(bf16[1024,512]{1,0:T(8,128)(2,1)} %param.10) | copy-start | bytes 3145732
  170.0 59.5 %copy-start.3 = (bf16[16,512]{1,0:T(8,128)(2,1)S(1)}, bf16[16,512]{1,0:T(8,128)(2,1)}, u32[]{:S(2)}) copy-start(bf16[16,512]{1,0:T(8,128)(2,1)} %param.7) | copy-start | bytes 49156
Sparse Core Ops, SparseCore 0:
  21.9 139.2 all-reduce.2
  193.3 36.1 reduce-scatter.1
